TPU v7x, 256 devices: a whole 4x4x8 slice. The times are simulated.
256 devices in a mesh: rows: 64 (over z, y, x_lo), cols: 4 (over x_hi, core).
Axes of the slice: x: 4 (x_hi: 2, x_lo: 2; x = x_hi * 2 + x_lo), y: 4, z: 8, core: 2. Of those that a mesh axis runs over, the one named last changes fastest.
Arguments:
- h_start: float32 [32768, 128], P(('rows', 'cols')), may hold values from -6 to 6
- cotangent: float32 [32768, 128], P(('rows', 'cols')), may hold values from -6 to 6
- node_type: int32 [32768], P(('rows', 'cols')), may hold values from 0 to 7
- teleport: float32 [8], replicated, may hold values from 0.05 to 0.5
- tile_values: bfloat16 [64, 4, 192, 128, 128], P('rows', 'cols'), may hold values from -0.0390625 to 0.0390625
- tile_row: int32 [64, 4, 192], P('rows', 'cols'), may hold values from 0 to 3, as said below
- tile_col: int32 [64, 4, 192], P('rows', 'cols'), may hold values from 0 to 63
- tile_count: int32 [64, 4], P('rows', 'cols'), may hold values from 24 to 192, as said below
Outputs:
- propagated: float32 [32768, 128], P(('rows', 'cols'))
- input_grad: float32 [32768, 128], P(('rows', 'cols'))
Inputs may be any that keep to these rules, and one draw needn't show every extreme that they name: Within one row block and column range, the pairs (tile_row, tile_col) of the 192 slots are all different. `tile_count`: slots at or beyond the count are not part of A. In every draw 4 row blocks use all 192 slots in every column range.
All inputs are finite; a program needn't handle non-finite values.
Results may differ from a plain program's by a relative error of at most 0.0029.
Values may be sent and summed in bfloat16 or wider, within the bound.
A program may use at most 64 MiB of HBM per device.

v0:
```python
import jax
import jax.numpy as jnp
from jax import lax
from jax.sharding import PartitionSpec as P

SLOT_BLOCK = 24


def tile_pass(
    tile_data,
    slot_rows,
    slot_cols,
    slot_count,
    panel_tiles,
    block_tiles,
    row_tiles,
    col_start,
    col_window,
):
    tile_size = tile_data.shape[-1]
    features = (panel_tiles if panel_tiles is not None else block_tiles).shape[-1]
    slot_total = tile_data.shape[0]
    running = []
    if panel_tiles is not None:
        running.append(jnp.zeros((row_tiles + 1, tile_size, features), jnp.float32))
    if block_tiles is not None:
        running.append(jnp.zeros((col_window + 1, tile_size, features), jnp.float32))
    block_count = (slot_count + SLOT_BLOCK - 1) // SLOT_BLOCK

    def advance(block_index, totals):
        slot_ids = block_index * SLOT_BLOCK + jnp.arange(SLOT_BLOCK, dtype=jnp.int32)
        active = slot_ids < slot_count
        where_at = jnp.clip(slot_ids, 0, slot_total - 1)
        values = jnp.take(tile_data, where_at, axis=0)
        row_ids = jnp.take(slot_rows, where_at)
        col_ids = jnp.take(slot_cols, where_at)
        updated = list(totals)
        if panel_tiles is not None:
            fetched = jnp.take(panel_tiles, col_ids, axis=0)
            product = jnp.einsum(
                "sij,sjf->sif", values, fetched, preferred_element_type=jnp.float32
            )
            segment = jnp.where(active, row_ids, row_tiles)
            updated[0] = totals[0].at[segment].add(product)
        if block_tiles is not None:
            fetched = jnp.take(block_tiles, row_ids, axis=0)
            product = jnp.einsum(
                "sji,sjf->sif", values, fetched, preferred_element_type=jnp.float32
            )
            local_col = col_ids - col_start
            inside = active & (local_col >= 0) & (local_col < col_window)
            segment = jnp.where(inside, local_col, col_window)
            updated[-1] = totals[-1].at[segment].add(product)
        return tuple(updated)

    totals = lax.fori_loop(0, block_count, advance, tuple(running))
    return [entry[:-1] for entry in totals]


def shards(h_start, cotangent, node_type, teleport, tile_values, tile_row, tile_col, tile_count):
    tile_data = tile_values[0, 0]
    slot_rows = tile_row[0, 0]
    slot_cols = tile_col[0, 0]
    slot_count = tile_count[0, 0]
    tile_size = tile_data.shape[-1]
    features = h_start.shape[-1]
    local_tiles = h_start.shape[0] // tile_size
    row_tiles = lax.axis_size("cols") * local_tiles
    col_tiles = lax.axis_size("rows") * local_tiles
    type_ids = jnp.arange(teleport.shape[0], dtype=jnp.int32)
    teleport_rate = jnp.sum(
        jnp.where(node_type[:, None] == type_ids[None, :], teleport[None, :], 0.0), axis=1
    )[:, None]
    keep_rate = 1.0 - teleport_rate

    def run_tiles(panel_tiles, block_tiles, col_start, col_window):
        return tile_pass(
            tile_data,
            slot_rows,
            slot_cols,
            slot_count,
            panel_tiles,
            block_tiles,
            row_tiles,
            col_start,
            col_window,
        )

    def gather_panel(local_part):
        gathered = lax.all_gather(local_part, "rows", axis=0, tiled=True)
        return gathered.reshape(col_tiles, tile_size, features)

    def gather_block(local_part):
        gathered = lax.all_gather(local_part, "cols", axis=0, tiled=True)
        return gathered.reshape(row_tiles, tile_size, features)

    def finish_forward(partial_value):
        return lax.psum_scatter(
            partial_value.reshape(row_tiles * tile_size, features),
            "cols",
            scatter_dimension=0,
            tiled=True,
        )

    def finish_adjoint(partial_value):
        return lax.psum_scatter(
            partial_value.reshape(col_tiles * tile_size, features),
            "rows",
            scatter_dimension=0,
            tiled=True,
        )

    def forward_hop(local_part):
        return finish_forward(run_tiles(gather_panel(local_part), None, 0, col_tiles)[0])

    first_panel = h_start.astype(jnp.bfloat16)
    first_adjoint = (keep_rate * cotangent).astype(jnp.bfloat16)
    hop_one = keep_rate * forward_hop(first_panel) + teleport_rate * h_start
    propagated = keep_rate * forward_hop(hop_one.astype(jnp.bfloat16)) + teleport_rate * h_start
    back_one = finish_adjoint(run_tiles(None, gather_block(first_adjoint), 0, col_tiles)[0])
    back_two = finish_adjoint(
        run_tiles(None, gather_block((keep_rate * back_one).astype(jnp.bfloat16)), 0, col_tiles)[0]
    )
    input_grad = teleport_rate * cotangent + teleport_rate * back_one + back_two
    return (propagated, input_grad)


def solution(mesh):
    placed = (
        P(("rows", "cols"), None),
        P(("rows", "cols"), None),
        P(("rows", "cols")),
        P(),
        P("rows", "cols", None, None, None),
        P("rows", "cols", None),
        P("rows", "cols", None),
        P("rows", "cols"),
    )
    return jax.shard_map(
        shards,
        mesh=mesh,
        in_specs=placed,
        out_specs=(P(("rows", "cols"), None), P(("rows", "cols"), None)),
        check_vma=False,
    )
```

profile of v0, /device:TPU:4, one launch (start us, length us, event | category | flops | bytes accessed | tf_op | source)
XLA Modules:
  0.0 1677.2 jit_solution(6281304382665034244)
XLA Ops:
  11.1 6.9 all_gather.14
  18.0 294.6 %all-gather.3.cloned.1.call-done = bf16[8192,128]{1,0:T(8,128)(2,1)} async-done(((bf16[128,128]{1,0:T(8,128)(2,1)}), bf16[8192,128]{1,0:T(8,128)(2,1)}) %all-gather.3.cloned.1.call-update) | async-done | bytes 2097168 | tf_op jit(solution)/shard_map/all_gather | solution.py:90
  312.6 41.1 %while.40 = (s32[]{:T(128)}, f32[5,128,128]{2,1,0:T(8,128)S(1)}, s32[]{:T(128)}, s32[]{:T(128)}, s32[192]{0:T(256)}, /*index=5*/bf16[192,128,128]{2,1,0:T(8,128)...) while((s32[]{:T(128)}, f32[5,128,128]{2,1,0:T(8,128)S(1)}, s32[]{:T(128)}, ...), condition=%wide.region_3.7_spmd, body=%wide.region_1.6_spmd.sunk | while | flops 101845808 | bytes 11023101 | solution.py:56
  314.1 2.3 gather_fusion.2
  316.4 4.3 gather_fusion.3
  323.7 2.6 scatter_fusion
  327.8 2.3 gather_fusion.2
  330.1 4.3 gather_fusion.3
  337.4 2.6 scatter_fusion
  341.5 2.3 gather_fusion.2
  343.8 4.3 gather_fusion.3
  351.1 2.6 scatter_fusion
  354.6 2.5 broadcast.91.clone
  357.1 39.4 %while.42 = (s32[]{:T(128)}, f32[65,128,128]{2,1,0:T(8,128)}, s32[]{:T(128)}, s32[]{:T(128)}, s32[192]{0:T(256)S(1)}, /*index=5*/bf16[192,128,128]{2,1,0:T(8,128...) while((s32[]{:T(128)}, f32[65,128,128]{2,1,0:T(8,128)}, s32[]{:T(128)}, ...), condition=%wide.region_11.16_spmd, body=%wide.region_9.15_spmd.sunk | while | flops 101845904 | bytes 11020001 | solution.py:56
  358.6 3.5 gather_fusion.11
  364.0 6.2 scatter_fusion.2
  371.6 3.5 gather_fusion.11
  377.0 6.2 scatter_fusion.2
  384.7 3.5 gather_fusion.11
  390.0 6.5 scatter_fusion.2
  396.6 4.7 slice.14
  401.3 39.3 %reduce-scatter.5.cloned.1.call-done = f32[128,128]{1,0:T(8,128)} async-done(((f32[512,128]{1,0:T(8,128)}), f32[128,128]{1,0:T(8,128)}) %reduce-scatter.5.cloned.1.call-update) | async-done | bytes 65552 | tf_op jit(solution)/shard_map/reduce_scatter | solution.py:98
  440.6 404.1 %reduce-scatter.9.cloned.1.call-done = f32[128,128]{1,0:T(8,128)} async-done(((f32[8192,128]{1,0:T(8,128)}), f32[128,128]{1,0:T(8,128)}) %reduce-scatter.9.cloned.1.call-update) | async-done | bytes 65552 | tf_op jit(solution)/shard_map/reduce_scatter | solution.py:106
  844.7 1.6 multiply_convert_fusion
  846.4 6.9 all_gather.15
  853.3 289.3 %all-gather.5.cloned.1.call-done = bf16[8192,128]{1,0:T(8,128)(2,1)} async-done(((bf16[128,128]{1,0:T(8,128)(2,1)}), bf16[8192,128]{1,0:T(8,128)(2,1)}) %all-gather.5.cloned.1.call-update) | async-done | bytes 2097168 | tf_op jit(solution)/shard_map/all_gather | solution.py:90
  1142.6 39.0 %while.41 = (s32[]{:T(128)}, f32[5,128,128]{2,1,0:T(8,128)S(1)}, s32[]{:T(128)}, s32[]{:T(128)}, s32[192]{0:T(256)S(1)}, /*index=5*/bf16[192,128,128]{2,1,0:T(8,...) while((s32[]{:T(128)}, f32[5,128,128]{2,1,0:T(8,128)S(1)}, s32[]{:T(128)}, ...), condition=%wide.region_7.11_spmd, body=%wide.region_5.10_spmd.sunk | while | flops 101845808 | bytes 11020001 | solution.py:56
  1143.4 2.3 gather_fusion.6
  1145.7 4.3 gather_fusion.7
  1153.0 2.6 scatter_fusion.1
  1156.4 2.3 gather_fusion.6
  1158.7 4.3 gather_fusion.7
  1166.0 2.6 scatter_fusion.1
  1169.4 2.3 gather_fusion.6
  1171.7 4.3 gather_fusion.7
  1179.0 2.6 scatter_fusion.1
  1182.4 2.5 broadcast.91
  1184.9 39.4 %while.43 = (s32[]{:T(128)}, f32[65,128,128]{2,1,0:T(8,128)}, s32[]{:T(128)}, s32[]{:T(128)}, s32[192]{0:T(256)S(1)}, /*index=5*/bf16[192,128,128]{2,1,0:T(8,128...) while((s32[]{:T(128)}, f32[65,128,128]{2,1,0:T(8,128)}, s32[]{:T(128)}, ...), condition=%wide.region_15.20_spmd, body=%wide.region_13.19_spmd.sunk | while | flops 101845904 | bytes 11020001 | solution.py:56
  1186.4 3.5 gather_fusion.15
  1191.8 6.2 scatter_fusion.3
  1199.4 3.5 gather_fusion.15
  1204.8 6.2 scatter_fusion.3
  1212.5 3.5 gather_fusion.15
  1217.8 6.5 scatter_fusion.3
  1224.4 4.7 slice.15
  1229.0 35.8 %reduce-scatter.7.cloned.1.call-done = f32[128,128]{1,0:T(8,128)} async-done(((f32[512,128]{1,0:T(8,128)}), f32[128,128]{1,0:T(8,128)}) %reduce-scatter.7.cloned.1.call-update) | async-done | bytes 65552 | tf_op jit(solution)/shard_map/reduce_scatter | solution.py:98
  1264.9 403.9 %reduce-scatter.11.cloned.1.call-done = f32[128,128]{1,0:T(8,128)} async-done(((f32[8192,128]{1,0:T(8,128)}), f32[128,128]{1,0:T(8,128)}) %reduce-scatter.11.cloned.1.call-update) | async-done | bytes 65552 | tf_op jit(solution)/shard_map/reduce_scatter | solution.py:106
  1668.8 1.6 multiply_add_fusion
  (138 shorter events, 49.1 us)
Async XLA Ops:
  7.2 305.5 %all-gather.3.cloned.1.call-start = ((), (), s32[]{:S(2)}) async-start(), calls=%async_computation.4 | async-start | bytes 2129920 | tf_op jit(solution)/shard_map/all_gather | solution.py:90
  8.7 431.9 %reduce-scatter.5.cloned.1.call-start = ((), (), s32[]{:S(2)}) async-start(), calls=%async_computation.5 | async-start | bytes 327680 | tf_op jit(solution)/shard_map/reduce_scatter | solution.py:98
  316.4 5.9 copy-start
  330.1 5.9 copy-start
  343.8 5.9 copy-start
  354.6 490.1 %reduce-scatter.9.cloned.1.call-start = ((), (), s32[]{:S(2)}) async-start(), calls=%async_computation.8 | async-start | bytes 4259840 | tf_op jit(solution)/shard_map/reduce_scatter | solution.py:106
  354.6 2.5 copy-start.1
  354.6 2.5 copy-start.2
  401.2 443.5 %copy-start.3 = (f32[128,128]{1,0:T(8,128)S(1)}, f32[128,128]{1,0:T(8,128)}, u32[]{:S(2)}) copy-start(f32[128,128]{1,0:T(8,128)} %param.24) | copy-start | bytes 196612
  401.2 741.3 %all-gather.5.cloned.1.call-start = ((), (), s32[]{:S(2)}) async-start(), calls=%async_computation.6 | async-start | bytes 2129920 | tf_op jit(solution)/shard_map/all_gather | solution.py:90
  846.3 418.6 %reduce-scatter.7.cloned.1.call-start = ((), (), s32[]{:S(2)}) async-start(), calls=%async_computation.7 | async-start | bytes 327680 | tf_op jit(solution)/shard_map/reduce_scatter | solution.py:98
  1182.4 486.4 %reduce-scatter.11.cloned.1.call-start = ((), (), s32[]{:S(2)}) async-start(), calls=%async_computation.9 | async-start | bytes 4259840 | tf_op jit(solution)/shard_map/reduce_scatter | solution.py:106
  1229.0 439.7 %copy-start.4 = (f32[128,128]{1,0:T(8,128)S(1)}, f32[128,128]{1,0:T(8,128)}, u32[]{:S(2)}) copy-start(f32[128,128]{1,0:T(8,128)} %param.25) | copy-start | bytes 196612
  1229.0 439.7 %copy-start.5 = (f32[128,128]{1,0:T(8,128)S(1)}, f32[128,128]{1,0:T(8,128)}, u32[]{:S(2)}) copy-start(f32[128,128]{1,0:T(8,128)} %reduce-scatter.9.cloned.1.call-done) | copy-start | bytes 196612
Sparse Core Ops, SparseCore 0:
  10.4 302.2 all-gather.2
  354.7 85.8 reduce-scatter.4
  443.3 401.3 reduce-scatter.8
  846.9 295.6 all-gather.4
  1182.5 82.3 reduce-scatter.6
  1267.4 401.2 reduce-scatter.10
where the time goes:
time: 1690 us; the launch traced here: 1680 us
  waiting for transfers between devices  1470 us (87%)
  local copies, waits for them, and re-layouts  99.7 us (6%)
  other arithmetic  68.2 us (4%)
    reduce_scatter x2, waiting for transfers between devices, finish_adjoint(): lax.psum_scatter(partial_value.reshape(col_tiles * tile_size, features),...  808 us
    all_gather x2, waiting for transfers between devices, gather_panel(): gathered = lax.all_gather(local_part, 'rows', axis=0, tiled=True)  584 us
    reduce_scatter x2, waiting for transfers between devices, finish_forward(): lax.psum_scatter(partial_value.reshape(row_tiles * tile_size, features),...  75.1 us
    gather x12, local copies, waits for them, and re-layouts, advance(): values = jnp.take(tile_data, where_at, axis=0)  46.9 us
    scatter-add x6, other arithmetic, advance(): updated[-1] = totals[-1].at[segment].add(product)  37.7 us
  transfers between devices with their start and end apart: 6, of which 6 were waited for; matrix products, arithmetic and copies ran while one was open for 6% of the time, Pallas kernels for 0%

commit v1 on v0

v1 whole, which is shorter than its diff:
```python
import functools

import jax
import jax.numpy as jnp
from jax import lax
from jax.experimental import pallas as pl
from jax.experimental.pallas import tpu as pltpu
from jax.sharding import PartitionSpec as P

MESH = pl.DeviceIdType.MESH
T = 128
NZ, NY = 8, 4
COLS = 4
GROUPS = 16
SLOTS = 192
CODED = True
MSG = jnp.int16 if CODED else jnp.float32
PAD = 16 if CODED else 0


def rem(a, n):
    return lax.rem(a + 2 * n, n)


def message_rows():
    offsets, total = {}, 0
    for name, steps, rows in (("az", NZ // 2, 4 * T), ("by", NY // 2, 8 * T), ("bz", NZ // 2, T), ("ay", NY // 2, T), ("x", 1, T)):
        for step in range(1, steps + 1):
            size = rows // 2 if (step == 1 and steps > 1) else rows
            offsets[name, step] = total
            total += size + PAD
    return offsets, total


OFFSETS, MSG_ROWS = message_rows()


def kernel(
    inv, tiles, h, cot, t_col, t_row, prop, grad,
    tv, ad, panel, part, qcat, acc, fsend1, frecv1, fsend2, frecv2, sbuf, rbuf, d_one,
    load_sem, ssem, rsem,
):
    r = lax.axis_index("rows")
    c = lax.axis_index("cols")
    z, y, x = r // 8, lax.rem(r // 2, 4), lax.rem(r, 2)
    xh, core = c // 2, lax.rem(c, 2)

    def at(zz, yy, xx):
        return {"rows": zz * 8 + yy * 2 + xx, "cols": c}

    zp, zm = at(rem(z + 1, NZ), y, x), at(rem(z - 1, NZ), y, x)
    yp, ym = at(z, rem(y + 1, NY), x), at(z, rem(y - 1, NY), x)
    xo = at(z, y, 1 - x)
    c_core = {"rows": r, "cols": xh * 2 + 1 - core}
    c_xh = {"rows": r, "cols": (1 - xh) * 2 + core}
    c_far = {"rows": r, "cols": (1 - xh) * 2 + 1 - core}

    load = pltpu.make_async_copy(tiles, tv.at[pl.ds(0, SLOTS)], load_sem)
    load.start()

    barrier = pltpu.get_barrier_semaphore()
    for peer in (zp, zm, yp, ym, xo, c_core, c_xh, c_far):
        pl.semaphore_signal(barrier, inc=1, device_id=peer, device_id_type=MESH)
    pl.semaphore_wait(barrier, 8)

    counter = [0]
    sent = []

    def remote(src, dst, peer):
        k = counter[0]
        counter[0] += 1
        copy = pltpu.make_async_remote_copy(
            src_ref=src, dst_ref=dst, send_sem=ssem.at[k], recv_sem=rsem.at[k],
            device_id=peer, device_id_type=MESH,
        )
        sent.append(copy)
        return copy

    own = jnp.where(x == 0, z * 4 + y, 32 + y * 8 + z)
    other = jnp.where(x == 0, 32 + y * 8 + z, z * 4 + y)

    def rows_of(start, size):
        return pl.ds(pl.multiple_of(start, 64), size)

    class Gather:
        def __init__(self, buf, n, pos, base, rows, plus, minus):
            self.buf, self.n, self.pos, self.base, self.rows = buf, n, pos, base, rows
            self.plus, self.minus, self.steps, self.waits = plus, minus, n // 2, {}

        def span(self, block, half):
            start = self.base + rem(block, self.n) * self.rows
            if half is None:
                return self.buf.at[rows_of(start, self.rows)]
            size = self.rows // 2
            return self.buf.at[rows_of(start + half * size, size)]

        def start(self, s):
            last = s == self.steps
            up = self.span(self.pos - (s - 1), 0 if last else None)
            down = self.span(self.pos + (s - 1), 1 if last else None)
            a, b = remote(up, up, self.plus), remote(down, down, self.minus)
            a.start()
            b.start()
            self.waits[s] = (a, b)

        def wait(self, s):
            for copy in self.waits[s]:
                copy.wait_recv()

    class Reduce:
        def __init__(self, hop, name, n, pos, base, rows, plus, minus):
            self.hop, self.name, self.n, self.pos, self.base, self.rows = hop, name, n, pos, base, rows
            self.plus, self.minus, self.steps, self.waits = plus, minus, n // 2, {}

        def start_row(self, block, half):
            return self.base + rem(block, self.n) * self.rows + (0 if half is None else half * (self.rows // 2))

        def send(self, s):
            s_rows = self.rows // 2 if s == 1 else self.rows
            off = OFFSETS[self.name, s]
            copies = []
            if s > 1:
                for copy in self.waits[s - 1]:
                    copy.wait_recv()
            for way, peer in ((0, self.minus), (1, self.plus)):
                block = self.pos - (self.steps + 1 - s) if way == 0 else self.pos + (self.steps + 1 - s)
                row = self.start_row(block, way if s == 1 else None)
                if s > 1:
                    p_rows = self.rows // 2 if s == 2 else self.rows
                    p_row = self.start_row(block, way if s == 2 else None)
                    add_message(self.hop, way, OFFSETS[self.name, s - 1], p_row, p_rows)
                pack_message(self.hop, way, off, row, s_rows)
                size = s_rows + PAD
                copy = remote(sbuf.at[self.hop, way, pl.ds(off, size)], rbuf.at[self.hop, way, pl.ds(off, size)], peer)
                copy.start()
                copies.append(copy)
            self.waits[s] = copies

        def finish(self):
            for way, copy in enumerate(self.waits[self.steps]):
                copy.wait_recv()
                add_message(self.hop, way, OFFSETS[self.name, self.steps], self.start_row(self.pos, None), self.rows)

    def add_message(hop, way, off, row, rows):
        step = min(rows, T)
        if CODED:
            e = rbuf[hop, way, pl.ds(off + rows, 16), :].astype(jnp.int32).astype(jnp.float32)
            scale = jnp.exp2(e - 14.0)[None, 0:8, :]

        def one(i, carry):
            src = rbuf[hop, way, pl.ds(pl.multiple_of(off + i * step, 16), step), :]
            if CODED:
                val = src.astype(jnp.int32).astype(jnp.float32).reshape(step // 8, 8, T) * scale
                val = val.reshape(step, T)
            else:
                val = src
            where = rows_of(row + i * step, step)
            part[where, :] = part[where, :] + val
            return carry

        lax.fori_loop(0, rows // step, one, 0)

    def pack_message(hop, way, off, row, rows):
        step = min(rows, T)
        if CODED:
            def largest(i, m):
                a = jnp.abs(part[rows_of(row + i * step, step), :]).reshape(step // 8, 8, T)
                return jnp.maximum(m, jnp.max(a, axis=0))

            m = lax.fori_loop(0, rows // step, largest, jnp.full((8, T), 1e-30, jnp.float32))
            m = jnp.max(m, axis=0, keepdims=True)
            e = jnp.ceil(jnp.log2(m))
            scale = jnp.broadcast_to(jnp.exp2(14.0 - e), (8, T))[None]
            sbuf[hop, way, pl.ds(off + rows, 16), :] = jnp.broadcast_to(e, (16, T)).astype(jnp.int32).astype(jnp.int16)

        def one(i, carry):
            a = part[rows_of(row + i * step, step), :]
            if CODED:
                a = jnp.round(a.reshape(step // 8, 8, T) * scale).reshape(step, T)
                a = a.astype(jnp.int32).astype(jnp.int16)
            sbuf[hop, way, pl.ds(pl.multiple_of(off + i * step, 16), step), :] = a
            return carry

        lax.fori_loop(0, rows // step, one, 0)

    def product_adjoint(hop, group):
        res = jnp.dot(qcat[hop], ad[group], preferred_element_type=jnp.float32)
        for i in range(4):
            part[rows_of(group * 512 + i * T, T), :] = res[:, i * T:(i + 1) * T]

    def product_forward(hop, group):
        acc[...] += jnp.dot(
            ad[group], panel[hop, rows_of(group * 512, 512), :], preferred_element_type=jnp.float32
        )

    def each(fn, hop, groups):
        def one(i, carry):
            g = groups[-1]
            for k in range(len(groups) - 1):
                g = jnp.where(i == k, groups[k], g)
            fn(hop, g)
            return carry

        lax.fori_loop(0, len(groups), one, 0)

    def az_groups(s):
        return [rem(z - s, NZ), rem(z + s, NZ)] if 0 < s < NZ // 2 else [rem(z + s, NZ)]

    def by_groups(s):
        blocks = [rem(y - s, NY), rem(y + s, NY)] if 0 < s < NY // 2 else [rem(y + s, NY)]
        return [8 + 2 * b + i for b in blocks for i in range(2)]

    cot_t = jnp.transpose(cot[...])
    keep_col = 1.0 - t_col[...]
    keep_row = 1.0 - t_row[...]
    lane = pl.ds(pl.multiple_of(c * T, T), T)
    tile_rows = rows_of(own * T, T)
    panel[0, tile_rows, :] = h[...].astype(jnp.bfloat16)
    qcat[0, :, lane] = (keep_row * cot_t).astype(jnp.bfloat16)

    def start_gather(hop):
        buf = panel.at[hop]
        first = remote(buf.at[tile_rows], buf.at[tile_rows], xo)
        first.start()
        return (
            first,
            Gather(buf, NY, y, z * 4 * T, T, yp, ym),
            Gather(buf, NZ, z, (32 + y * 8) * T, T, zp, zm),
            Gather(buf, NZ, z, 0, 4 * T, zp, zm),
            Gather(buf, NY, y, 32 * T, 8 * T, yp, ym),
        )

    def start_cols(hop):
        copies = []
        for peer in (c_core, c_xh, c_far):
            copy = remote(qcat.at[hop, :, lane], qcat.at[hop, :, lane], peer)
            copy.start()
            copies.append(copy)
        return copies

    for hop in range(2):
        first, g_ay, g_bz, g_az, g_by = start_gather(hop)
        q_copies = start_cols(hop)
        az = Reduce(hop, "az", NZ, z, 0, 4 * T, zp, zm)
        by = Reduce(hop, "by", NY, y, 32 * T, 8 * T, yp, ym)
        bz = Reduce(hop, "bz", NZ, z, (32 + y * 8) * T, T, zp, zm)
        ay = Reduce(hop, "ay", NY, y, z * 4 * T, T, yp, ym)

        if hop == 0:
            load.wait()
            tv[SLOTS] = jnp.zeros((T, T), jnp.bfloat16)

            def fill(g, carry):
                for q in range(COLS):
                    for i in range(4):
                        ad[g, q * T:(q + 1) * T, i * T:(i + 1) * T] = tv[inv[q * 64 + g * 4 + i]]
                return carry

            lax.fori_loop(0, GROUPS, fill, 0)
        acc[...] = jnp.zeros_like(acc)

        first.wait_recv()
        g_ay.start(1)
        g_bz.start(1)
        for copy in q_copies:
            copy.wait_recv()
        each(product_adjoint, hop, az_groups(4) + by_groups(2))
        az.send(1)
        by.send(1)
        g_ay.wait(1)
        g_ay.start(2)
        g_bz.wait(1)
        g_bz.start(2)
        each(product_adjoint, hop, az_groups(3) + by_groups(1))
        az.send(2)
        by.send(2)
        g_ay.wait(2)
        g_az.start(1)
        g_bz.wait(2)
        g_bz.start(3)
        each(product_adjoint, hop, az_groups(2) + by_groups(0))
        az.send(3)
        by.finish()
        bz.send(1)
        g_az.wait(1)
        g_az.start(2)
        g_bz.wait(3)
        g_bz.start(4)
        each(product_adjoint, hop, az_groups(1) + az_groups(0))
        az.send(4)
        bz.send(2)
        g_bz.wait(4)
        g_by.start(1)
        each(product_forward, hop, az_groups(0) + az_groups(1))
        g_az.wait(2)
        g_az.start(3)
        az.finish()
        ay.send(1)
        bz.send(3)
        each(product_forward, hop, az_groups(2) + by_groups(0))
        g_by.wait(1)
        g_by.start(2)
        g_az.wait(3)
        g_az.start(4)
        ay.send(2)
        bz.send(4)
        each(product_forward, hop, az_groups(3) + by_groups(1))
        ay.finish()
        bz.finish()
        off = OFFSETS["x", 1]
        pack_message(hop, 0, off, other * T, T)
        x_copy = remote(
            sbuf.at[hop, 0, pl.ds(off, T + PAD)], rbuf.at[hop, 0, pl.ds(off, T + PAD)], xo
        )
        x_copy.start()
        g_az.wait(4)
        g_by.wait(2)
        each(product_forward, hop, az_groups(4) + by_groups(2))

        for i in range(2):
            fsend1[hop, i] = acc[rows_of((2 * i + 1 - core) * T, T), :]
        f_core = remote(fsend1.at[hop], frecv1.at[hop], c_core)
        f_core.start()
        x_copy.wait_recv()
        add_message(hop, 0, off, own * T, T)
        d = part[tile_rows, :]
        if hop == 0:
            d_one[...] = d
            qcat[1, :, lane] = (keep_row * d).astype(jnp.bfloat16)
        else:
            grad[...] = jnp.transpose(t_row[...] * cot_t + t_row[...] * d_one[...] + d)
        f_core.wait_recv()
        fsend2[hop] = acc[rows_of((2 * (1 - xh) + core) * T, T), :] + frecv1[hop, 1 - xh]
        f_xh = remote(fsend2.at[hop], frecv2.at[hop], c_xh)
        f_xh.start()
        mine = acc[rows_of((2 * xh + core) * T, T), :] + frecv1[hop, xh]
        f_xh.wait_recv()
        mine = keep_col * (mine + frecv2[hop]) + t_col[...] * h[...]
        if hop == 0:
            panel[1, tile_rows, :] = mine.astype(jnp.bfloat16)
        else:
            prop[...] = mine

    for copy in sent:
        copy.wait_send()


def shards(h_start, cotangent, node_type, teleport, tile_values, tile_row, tile_col, tile_count):
    type_ids = jnp.arange(teleport.shape[0], dtype=jnp.int32)
    rate = jnp.sum(jnp.where(node_type[:, None] == type_ids[None, :], teleport[None, :], 0.0), axis=1)
    t_col = jnp.broadcast_to(rate[:, None], (T, T))
    t_row = rate[None, :]
    k = tile_col[0, 0]
    kz, ky, kx = k // 8, (k // 2) % 4, k % 2
    place = tile_row[0, 0] * 64 + jnp.where(kx == 0, kz * 4 + ky, 32 + ky * 8 + kz)
    slot = jnp.arange(SLOTS, dtype=jnp.int32)
    place = jnp.where(slot < tile_count[0, 0], place, -1)
    hit = place[None, :] == jnp.arange(COLS * 64, dtype=jnp.int32)[:, None]
    inv = SLOTS + jnp.sum(jnp.where(hit, slot[None, :] - SLOTS, 0), axis=1)

    vmem = pl.BlockSpec(memory_space=pltpu.VMEM)
    tile = jax.ShapeDtypeStruct((T, T), jnp.float32)
    copies = 112
    return pl.pallas_call(
        kernel,
        out_shape=(tile, tile),
        in_specs=[pl.BlockSpec(memory_space=pltpu.SMEM), pl.BlockSpec(memory_space=pl.ANY)] + [vmem] * 4,
        out_specs=(vmem, vmem),
        scratch_shapes=[
            pltpu.VMEM((SLOTS + 1, T, T), jnp.bfloat16),
            pltpu.VMEM((GROUPS, 512, 512), jnp.bfloat16),
            pltpu.VMEM((2, 64 * T, T), jnp.bfloat16),
            pltpu.VMEM((64 * T, T), jnp.float32),
            pltpu.VMEM((2, T, COLS * T), jnp.bfloat16),
            pltpu.VMEM((COLS * T, T), jnp.float32),
            pltpu.VMEM((2, 2, T, T), jnp.float32),
            pltpu.VMEM((2, 2, T, T), jnp.float32),
            pltpu.VMEM((2, T, T), jnp.float32),
            pltpu.VMEM((2, T, T), jnp.float32),
            pltpu.VMEM((2, 2, MSG_ROWS, T), MSG),
            pltpu.VMEM((2, 2, MSG_ROWS, T), MSG),
            pltpu.VMEM((T, T), jnp.float32),
            pltpu.SemaphoreType.DMA,
            pltpu.SemaphoreType.DMA((copies,)),
            pltpu.SemaphoreType.DMA((copies,)),
        ],
        compiler_params=pltpu.CompilerParams(
            collective_id=0, has_side_effects=True, vmem_limit_bytes=56 << 20
        ),
    )(inv, tile_values[0, 0], h_start, cotangent, t_col, t_row)


def solution(mesh):
    placed = (
        P(("rows", "cols"), None),
        P(("rows", "cols"), None),
        P(("rows", "cols")),
        P(),
        P("rows", "cols", None, None, None),
        P("rows", "cols", None),
        P("rows", "cols", None),
        P("rows", "cols"),
    )
    return jax.shard_map(
        shards,
        mesh=mesh,
        in_specs=placed,
        out_specs=(P(("rows", "cols"), None), P(("rows", "cols"), None)),
        check_vma=False,
    )
```

time: 1690 us -> 113 us (0.07)
  the two profiles are of different devices: /device:TPU:4 before, /device:TPU:1 now
where the time goes in v1:
time: 113 us; the launch traced here: 112 us
  Pallas kernels  105 us (93%)
  local copies, waits for them, and re-layouts  3.66 us (3%)
  other arithmetic  2.84 us (3%)
  between operations  1.29 us (1%)
    pallas_call x1, Pallas kernels, shards(): pl.pallas_call(kernel, out_shape=(tile, tile), in_specs=[pl.BlockSpec(mem...  105 us
    unnamed x4, local copies, waits for them, and re-layouts  2.95 us

profile of v1, /device:TPU:1, one launch (start us, length us, event | category | flops | bytes accessed | tf_op | source)
XLA Modules:
  0.0 112.4 jit_solution(17245301476717978700)
XLA Ops:
  1.3 0.8 select_reduce_fusion.1
  2.0 0.0 copy-start
  2.0 0.7 broadcast_multiply_fusion
  2.7 0.7 compare_select_fusion.3
  3.4 0.1 select_reduce_fusion
  3.5 0.6 broadcast_add_fusion.inv
  4.1 0.7 broadcast_in_dim.45.t_col
  4.8 0.0 copy-done
  4.8 104.6 %shard_map.95 = (f32[128,128]{1,0:T(8,128)}, f32[128,128]{1,0:T(8,128)}) custom-call(s32[256]{0:T(256)} %broadcast_add_fusion.inv, bf16[192,128,128]{2,1,0:T(8,128)(2,1)} %bitcast.6, f32[128,128]{1,0:T(8,128)} %h.1, f32[128,128]{1,0:T(8,128)} %cot.1, f32[128,128]{1,0:T(8,128)} %broadcast_in_dim.45.t_col, f32[1,128]{1,0:T(1,128)} %bitcast.8), custom_call_target="tpu_custom_call" | custom-call | tf_op jit(solution)/shard_map/pallas_call | solution.py:364
  109.4 1.5 %copy.13 = f32[128,128]{1,0:T(8,128)} copy(f32[128,128]{1,0:T(8,128)} %get-tuple-element.6) | data formatting | bytes 131072
  110.9 1.5 %copy.14 = f32[128,128]{1,0:T(8,128)} copy(f32[128,128]{1,0:T(8,128)} %get-tuple-element.7) | data formatting | bytes 131072
Async XLA Ops:
  2.0 2.8 %copy-start = (f32[128]{0:T(128)}, f32[128]{0:T(128)S(1)}, u32[]{:S(2)}) copy-start(f32[128]{0:T(128)S(1)} %select_reduce_fusion.1) | copy-start | bytes 1540

commit v2 on v0

v2 whole, which is shorter than its diff:
```python
import jax
import jax.numpy as jnp
from jax import lax
from jax.experimental import pallas as pl
from jax.experimental.pallas import tpu as pltpu
from jax.sharding import PartitionSpec as P

MESH = pl.DeviceIdType.MESH
T = 128
NZ, NY, NX = 8, 4, 2
COLS = 4
GROUPS = 16
SLOTS = 192
PAD = 16
PARTS = (2, 1, 3, 0)


def rem(a, n):
    return lax.rem(a + 2 * n, n)


def kernel(
    inv, rates, tiles, h, cot, types, prop, grad,
    tv, ad, panel, part, qcat, acc, fsend1, frecv1, fsend2, frecv2,
    s_one, r_one, s_two, r_two, s_x, r_x, s_own, r_own, d_one,
    load_sem, ssem, rsem, so, ro,
):
    r = lax.axis_index("rows")
    c = lax.axis_index("cols")
    z, y, x = r // 8, lax.rem(r // 2, 4), lax.rem(r, 2)
    xh, core = c // 2, lax.rem(c, 2)
    zpair = z // 2

    def at(zz, yy, xx):
        return {"rows": zz * 8 + yy * 2 + xx, "cols": c}

    zp, zm = at(rem(z + 1, NZ), y, x), at(rem(z - 1, NZ), y, x)
    yp, ym = at(z, rem(y + 1, NY), x), at(z, rem(y - 1, NY), x)
    c_core = {"rows": r, "cols": xh * 2 + 1 - core}
    c_xh = {"rows": r, "cols": (1 - xh) * 2 + core}
    c_far = {"rows": r, "cols": (1 - xh) * 2 + 1 - core}
    y_plane = [(dy, dx) for dy in (2, 1, 3, 0) for dx in (1, 0) if dy or dx]

    def in_y(dy, dx):
        return at(z, rem(y + dy, NY), 1 - x if dx else x)

    load = pltpu.make_async_copy(tiles, tv.at[pl.ds(0, SLOTS)], load_sem)
    load.start()

    barrier = pltpu.get_barrier_semaphore()
    peers = [in_y(*p) for p in y_plane] + [at(rem(z + d, NZ), y, x) for d in range(1, NZ)] + [c_core, c_xh, c_far]
    for peer in peers:
        pl.semaphore_signal(barrier, inc=1, device_id=peer, device_id_type=MESH)

    t_row = jnp.zeros((1, T), jnp.float32)
    for i in range(8):
        t_row = t_row + jnp.where(types[...] == i, rates[i], 0.0)
    keep_row = 1.0 - t_row
    lane = pl.ds(pl.multiple_of(c * T, T), T)
    panel[0, z, x, y] = h[...].astype(jnp.bfloat16)
    qcat[0, :, lane] = (keep_row * jnp.transpose(cot[...])).astype(jnp.bfloat16)

    counter = [0]
    sent = []

    def remote(src, dst, peer):
        k = counter[0]
        counter[0] += 1
        copy = pltpu.make_async_remote_copy(
            src_ref=src, dst_ref=dst, send_sem=ssem.at[k], recv_sem=rsem.at[k],
            device_id=peer, device_id_type=MESH,
        )
        copy.index = k
        sent.append(copy)
        return copy

    def landed(slot, copy):
        pltpu.make_async_remote_copy(
            src_ref=slot, dst_ref=slot, send_sem=ssem.at[copy.index], recv_sem=rsem.at[copy.index],
            device_id=yp, device_id_type=MESH,
        ).wait_recv()

    def rows_of(start, size):
        return pl.ds(pl.multiple_of(start, T), size)

    def each(fn, hop, groups):
        def one(i, carry):
            g = groups[-1]
            for k in range(len(groups) - 1):
                g = jnp.where(i == k, groups[k], g)
            fn(hop, g)
            return carry

        lax.fori_loop(0, len(groups), one, 0)

    def tile_row(dy, zz, xx):
        return (rem(y + dy, NY) * 16 + xx * 8 + zz) * T

    def product_adjoint(hop, g):
        res = jnp.dot(qcat[hop], ad[g], preferred_element_type=jnp.float32)
        for i in range(NY):
            part[rows_of((i * 16 + lax.rem(g, 2) * 8 + g // 2) * T, T), :] = res[:, i * T:(i + 1) * T]

    def product_forward(hop, g):
        tile4 = panel[hop, g // 2, lax.rem(g, 2)].reshape(NY * T, T)
        acc[...] += jnp.dot(ad[g], tile4, preferred_element_type=jnp.float32)

    def decode(msg, row, scale):
        val = msg[rows_of(row, T), :].astype(jnp.int32).astype(jnp.float32)
        return (val.reshape(T // 8, 8, T) * scale).reshape(T, T)

    def scale_of(msg, rows):
        e = msg[pl.ds(rows, PAD), :].astype(jnp.int32).astype(jnp.float32)
        return jnp.exp2(e - 14.0)[None, 0:8, :]

    def place(row, i):
        return rows_of(row + (i // 2) * 8 * T + lax.rem(i, 2) * T, T)

    def add_message(msg, row, tiles_in):
        scale = scale_of(msg, tiles_in * T)

        def one(i, carry):
            where = place(row, i)
            part[where, :] = part[where, :] + decode(msg, i * T, scale)
            return carry

        lax.fori_loop(0, tiles_in, one, 0)

    def pack_message(msg, row, tiles_in):
        def largest(i, m):
            a = jnp.abs(part[place(row, i), :]).reshape(T // 8, 8, T)
            return jnp.maximum(m, jnp.max(a, axis=0))

        m = lax.fori_loop(0, tiles_in, largest, jnp.full((8, T), 1e-30, jnp.float32))
        e = jnp.ceil(jnp.log2(jnp.max(m, axis=0, keepdims=True)))
        scale = jnp.broadcast_to(jnp.exp2(14.0 - e), (8, T))[None]
        msg[pl.ds(tiles_in * T, PAD), :] = jnp.broadcast_to(e, (PAD, T)).astype(jnp.int32).astype(jnp.int16)

        def one(i, carry):
            a = part[place(row, i), :].reshape(T // 8, 8, T)
            a = jnp.round(a * scale).reshape(T, T)
            msg[rows_of(i * T, T), :] = a.astype(jnp.int32).astype(jnp.int16)
            return carry

        lax.fori_loop(0, tiles_in, one, 0)


    planes = {}

    def plane_start(hop):
        own = panel.at[hop, z, x, y]
        for k, (dy, dx) in enumerate(y_plane):
            planes[hop, -dy % NY, dx] = remote(own, own, in_y(dy, dx))
            planes[hop, -dy % NY, dx].start()

    def plane_wait(hop, dx):
        for d in range(1 - dx, NY):
            slot = panel.at[hop, z, 1 - x if dx else x, rem(y + d, NY)]
            landed(slot, planes[hop, d, dx])

    rings = {}

    def ring(hop, i, s):
        if s > 1:
            for copy in rings[hop, i, s - 1]:
                copy.wait_recv()
        xx = 1 - x if i else x
        up, down = panel.at[hop, rem(z - (s - 1), NZ), xx], panel.at[hop, rem(z + (s - 1), NZ), xx]
        pairs = [(up, zp), (down, zm)]
        if s == NZ // 2:
            pairs = pairs[i:i + 1]
        rings[hop, i, s] = [remote(block, block, peer) for block, peer in pairs]
        for copy in rings[hop, i, s]:
            copy.start()

    def ring_products(hop, i, s):
        xx = 1 - x if i else x
        groups = [rem(z - s, NZ) * 2 + xx, rem(z + s, NZ) * 2 + xx]
        each(product_forward, hop, groups if 0 < s < NZ // 2 else groups[:1])

    forward = {}

    def forward_core(hop):
        for i in range(2):
            fsend1[hop, i] = acc[rows_of((2 * i + 1 - core) * T, T), :]
        forward["core", hop] = remote(fsend1.at[hop], frecv1.at[hop], c_core)
        forward["core", hop].start()

    def forward_far(hop):
        forward["core", hop].wait_recv()
        fsend2[hop] = acc[rows_of((2 * (1 - xh) + core) * T, T), :] + frecv1[hop, 1 - xh]
        forward["far", hop] = remote(fsend2.at[hop], frecv2.at[hop], c_xh)
        forward["far", hop].start()

    def forward_end(hop):
        mine = acc[rows_of((2 * xh + core) * T, T), :] + frecv1[hop, xh]
        t_col = jnp.transpose(jnp.broadcast_to(t_row, (T, T)))
        forward["far", hop].wait_recv()
        mine = (1.0 - t_col) * (mine + frecv2[hop]) + t_col * h[...]
        if hop == 0:
            panel[1, z, x, y] = mine.astype(jnp.bfloat16)
        else:
            prop[...] = mine


    queries = {}

    def query_start(hop):
        queries[hop] = [remote(qcat.at[hop, :, lane], qcat.at[hop, :, lane], peer) for peer in (c_far, c_xh, c_core)]
        for copy in queries[hop]:
            copy.start()

    def query_wait(hop):
        for copy in queries[hop]:
            copy.wait_recv()

    reduces = {}

    def pair(j):
        return 2 * rem(zpair + j, 4)

    def reduce_one(hop, j):
        zz = pair(j)
        each(product_adjoint, hop, [zz * 2 + i for i in range(4)])
        for way, peer in ((0, ym), (1, yp)):
            msg = s_one.at[hop, j, way]
            pack_message(msg, tile_row(2, zz, way), 2)
            copy = remote(msg, r_one.at[hop, j, way], peer)
            copy.start()
            reduces[1, hop, j, way] = copy

    def reduce_two(hop, j):
        zz = pair(j)
        for way, peer, dy in ((0, ym, -1), (1, yp, 1)):
            reduces[1, hop, j, way].wait_recv()
            add_message(r_one.at[hop, j, way], tile_row(dy, zz, way), 2)
            msg = s_two.at[hop, j, way]
            pack_message(msg, tile_row(dy, zz, 0), 4)
            copy = remote(msg, r_two.at[hop, j, way], peer)
            copy.start()
            reduces[2, hop, j, way] = copy

    def reduce_x(hop, j):
        zz = pair(j)
        for way in range(2):
            reduces[2, hop, j, way].wait_recv()
            add_message(r_two.at[hop, j, way], tile_row(0, zz, 0), 4)
        msg = s_x.at[hop, j]
        pack_message(msg, tile_row(0, zz, 1 - x), 2)
        reduces[3, hop, j] = remote(msg, r_x.at[hop, j], at(z, y, 1 - x))
        reduces[3, hop, j].start()

    def own_copy(hop, j, i):
        zz = pair(j) + i
        slot = rem(z - zz, NZ)
        copy = pltpu.make_async_remote_copy(
            src_ref=s_own.at[hop, j, i], dst_ref=r_own.at[hop, slot],
            send_sem=so.at[hop, 2 * j + i], recv_sem=ro.at[hop, slot],
            device_id=at(zz, y, x), device_id_type=MESH,
        )
        return copy, slot

    def reduce_own(hop, j):
        zz = pair(j)
        reduces[3, hop, j].wait_recv()
        add_message(r_x.at[hop, j], tile_row(0, zz, x), 2)
        for i in range(2):
            pack_message(s_own.at[hop, j, i], tile_row(0, zz + i, x), 1)
            copy, slot = own_copy(hop, j, i)
            if j:
                copy.start()
            else:
                pl.when(slot != 0)(copy.start)

    def own_done(hop):
        for j in range(4):
            for i in range(2):
                copy, slot = own_copy(hop, j, i)
                if j:
                    copy.wait_send()
                else:
                    pl.when(slot != 0)(copy.wait_send)

    def adjoint_end(hop):
        for slot in range(1, NZ):
            pltpu.make_async_remote_copy(
                src_ref=r_own.at[hop, slot], dst_ref=r_own.at[hop, slot], send_sem=so.at[hop, 0],
                recv_sem=ro.at[hop, slot], device_id=yp, device_id_type=MESH,
            ).wait_recv()

        row = tile_row(0, z, x)

        def one(slot, carry):
            add_message(r_own.at[hop, slot], row, 1)
            return carry

        lax.fori_loop(1, NZ, one, 0)
        d = part[rows_of(row, T), :]
        if hop == 0:
            d_one[...] = d
            qcat[1, :, lane] = (keep_row * d).astype(jnp.bfloat16)
        else:
            grad[...] = jnp.transpose(t_row * jnp.transpose(cot[...]) + t_row * d_one[...] + d)

    pl.semaphore_wait(barrier, len(peers))
    plane_start(0)
    query_start(0)
    load.wait()
    tv[SLOTS] = jnp.zeros((T, T), jnp.bfloat16)

    def fill(g, carry):
        for q in range(COLS):
            for i in range(4):
                ad[g, q * T:(q + 1) * T, i * T:(i + 1) * T] = tv[inv[q * 64 + g * 4 + i]]
        return carry

    lax.fori_loop(0, GROUPS, fill, 0)

    p = PARTS
    query_wait(0)
    acc[...] = jnp.zeros_like(acc)
    for hop in range(2):
        plane_wait(hop, 0)
        ring(hop, 0, 1)
        plane_wait(hop, 1)
        ring(hop, 1, 1)
        if hop == 0:
            reduce_one(hop, p[0])
            reduce_one(hop, p[1])
        ring_products(hop, 0, 0)
        ring(hop, 0, 2)
        if hop == 0:
            reduce_one(hop, p[2])
            reduce_one(hop, p[3])
        ring(hop, 1, 2)
        reduce_two(hop, p[0])
        reduce_two(hop, p[1])
        ring_products(hop, 1, 0)
        ring_products(hop, 0, 1)
        ring_products(hop, 1, 1)
        ring(hop, 0, 3)
        reduce_two(hop, p[2])
        ring(hop, 1, 3)
        reduce_x(hop, p[0])
        reduce_two(hop, p[3])
        ring_products(hop, 0, 2)
        ring_products(hop, 1, 2)
        reduce_x(hop, p[1])
        ring(hop, 0, 4)
        reduce_own(hop, p[0])
        ring(hop, 1, 4)
        reduce_x(hop, p[2])
        reduce_own(hop, p[1])
        ring_products(hop, 0, 3)
        ring_products(hop, 1, 3)
        reduce_x(hop, p[3])
        reduce_own(hop, p[2])
        for i in range(2):
            rings[hop, i, 4][0].wait_recv()
            ring_products(hop, i, 4)
        forward_core(hop)
        reduce_own(hop, p[3])
        forward_far(hop)
        adjoint_end(hop)
        if hop == 0:
            query_start(1)
        forward_end(hop)
        if hop == 0:
            plane_start(1)
            acc[...] = jnp.zeros_like(acc)
            query_wait(1)
            for j in p:
                reduce_one(1, j)

    for copy in sent:
        copy.wait_send()
    for hop in range(2):
        own_done(hop)


def shards(h_start, cotangent, node_type, teleport, tile_values, tile_row, tile_col, tile_count):
    k = tile_col[0, 0]
    place = tile_row[0, 0] * 64 + (k // 8 * 2 + k % 2) * 4 + (k // 2) % 4
    slot = jnp.arange(SLOTS, dtype=jnp.int32)
    place = jnp.where(slot < tile_count[0, 0], place, -1)
    hit = place[None, :] == jnp.arange(COLS * 64, dtype=jnp.int32)[:, None]
    inv = SLOTS + jnp.sum(jnp.where(hit, slot[None, :] - SLOTS, 0), axis=1)

    vmem = pl.BlockSpec(memory_space=pltpu.VMEM)
    smem = pl.BlockSpec(memory_space=pltpu.SMEM)
    tile = jax.ShapeDtypeStruct((T, T), jnp.float32)
    copies = 96
    return pl.pallas_call(
        kernel,
        out_shape=(tile, tile),
        in_specs=[smem, smem, pl.BlockSpec(memory_space=pl.ANY)] + [vmem] * 3,
        out_specs=(vmem, vmem),
        scratch_shapes=[
            pltpu.VMEM((SLOTS + 1, T, T), jnp.bfloat16),
            pltpu.VMEM((GROUPS, 512, 512), jnp.bfloat16),
            pltpu.VMEM((2, NZ, NX, NY, T, T), jnp.bfloat16),
            pltpu.VMEM((64 * T, T), jnp.float32),
            pltpu.VMEM((2, T, COLS * T), jnp.bfloat16),
            pltpu.VMEM((COLS * T, T), jnp.float32),
            pltpu.VMEM((2, 2, T, T), jnp.float32),
            pltpu.VMEM((2, 2, T, T), jnp.float32),
            pltpu.VMEM((2, T, T), jnp.float32),
            pltpu.VMEM((2, T, T), jnp.float32),
            pltpu.VMEM((2, 4, 2, 2 * T + PAD, T), jnp.int16),
            pltpu.VMEM((2, 4, 2, 2 * T + PAD, T), jnp.int16),
            pltpu.VMEM((2, 4, 2, 4 * T + PAD, T), jnp.int16),
            pltpu.VMEM((2, 4, 2, 4 * T + PAD, T), jnp.int16),
            pltpu.VMEM((2, 4, 2 * T + PAD, T), jnp.int16),
            pltpu.VMEM((2, 4, 2 * T + PAD, T), jnp.int16),
            pltpu.VMEM((2, 4, 2, T + PAD, T), jnp.int16),
            pltpu.VMEM((2, NZ, T + PAD, T), jnp.int16),
            pltpu.VMEM((T, T), jnp.float32),
            pltpu.SemaphoreType.DMA,
            pltpu.SemaphoreType.DMA((copies,)),
            pltpu.SemaphoreType.DMA((copies,)),
            pltpu.SemaphoreType.DMA((2, NZ)),
            pltpu.SemaphoreType.DMA((2, NZ)),
        ],
        compiler_params=pltpu.CompilerParams(
            collective_id=0, has_side_effects=True, vmem_limit_bytes=56 << 20
        ),
    )(inv, teleport, tile_values[0, 0], h_start, cotangent, node_type[None, :])


def solution(mesh):
    placed = (
        P(("rows", "cols"), None),
        P(("rows", "cols"), None),
        P(("rows", "cols")),
        P(),
        P("rows", "cols", None, None, None),
        P("rows", "cols", None),
        P("rows", "cols", None),
        P("rows", "cols"),
    )
    return jax.shard_map(
        shards,
        mesh=mesh,
        in_specs=placed,
        out_specs=(P(("rows", "cols"), None), P(("rows", "cols"), None)),
        check_vma=False,
    )
```

time: 1690 us -> 97.9 us (0.06)
  the two profiles are of different devices: /device:TPU:4 before, /device:TPU:1 now
where the time goes in v2:
time: 97.9 us; the launch traced here: 97.6 us
  Pallas kernels  91.3 us (93%)
  local copies, waits for them, and re-layouts  2.95 us (3%)
  other arithmetic  2.08 us (2%)
  between operations  1.29 us (1%)
    pallas_call x1, Pallas kernels, shards(): pl.pallas_call(kernel, out_shape=(tile, tile), in_specs=[smem, smem, pl.B...  91.3 us
    unnamed x2, local copies, waits for them, and re-layouts  2.95 us

profile of v2, /device:TPU:1, one launch (start us, length us, event | category | flops | bytes accessed | tf_op | source)
XLA Modules:
  0.0 97.6 jit_solution(966509704591040423)
XLA Ops:
  1.3 0.7 broadcast_multiply_fusion
  2.0 0.7 compare_select_fusion.2
  2.7 0.1 select_reduce_fusion
  2.8 0.6 broadcast_add_fusion.inv
  3.4 91.3 %shard_map.95 = (f32[128,128]{1,0:T(8,128)}, f32[128,128]{1,0:T(8,128)}) custom-call(s32[256]{0:T(256)} %broadcast_add_fusion.inv, f32[8]{0:T(128)} %rates.1, bf16[192,128,128]{2,1,0:T(8,128)(2,1)} %bitcast.6, f32[128,128]{1,0:T(8,128)} %h.1, f32[128,128]{1,0:T(8,128)} %cot.1, s32[1,128]{1,0:T(1,128)} %bitcast.9), custom_call_target="tpu_custom_call" | custom-call | tf_op jit(solution)/shard_map/pallas_call | solution.py:393
  94.7 1.5 %copy.13 = f32[128,128]{1,0:T(8,128)} copy(f32[128,128]{1,0:T(8,128)} %get-tuple-element.6) | data formatting | bytes 131072
  96.1 1.5 %copy.14 = f32[128,128]{1,0:T(8,128)} copy(f32[128,128]{1,0:T(8,128)} %get-tuple-element.7) | data formatting | bytes 131072

commit v3 on v2

--- a/solution.py
+++ b/solution.py
@@ -21,7 +21,7 @@
 
 def kernel(
     inv, rates, tiles, h, cot, types, prop, grad,
-    tv, ad, panel, part, qcat, acc, fsend1, frecv1, fsend2, frecv2,
+    tv, ad, panel, part, qcat, acc, s_cols, r_cols,
     s_one, r_one, s_two, r_two, s_x, r_x, s_own, r_own, d_one,
     load_sem, ssem, rsem, so, ro,
 ):
@@ -44,7 +44,7 @@
     def in_y(dy, dx):
         return at(z, rem(y + dy, NY), 1 - x if dx else x)
 
-    load = pltpu.make_async_copy(tiles, tv.at[pl.ds(0, SLOTS)], load_sem)
+    load = pltpu.make_async_copy(tiles, tv.at[pl.ds(1, SLOTS)], load_sem)
     load.start()
 
     barrier = pltpu.get_barrier_semaphore()
@@ -158,20 +158,45 @@
             slot = panel.at[hop, z, 1 - x if dx else x, rem(y + d, NY)]
             landed(slot, planes[hop, d, dx])
 
-    rings = {}
+    rings, crossed = {}, {}
 
     def ring(hop, i, s):
+        xx = x if i < 2 else 1 - x
+        part_of = pl.ds(2 * (i % 2), 2)
         if s > 1:
             for copy in rings[hop, i, s - 1]:
                 copy.wait_recv()
-        xx = 1 - x if i else x
-        up, down = panel.at[hop, rem(z - (s - 1), NZ), xx], panel.at[hop, rem(z + (s - 1), NZ), xx]
+        blocks = [rem(z - (s - 1), NZ), rem(z + (s - 1), NZ)]
+        up, down = [panel.at[hop, b, xx, part_of] for b in blocks]
         pairs = [(up, zp), (down, zm)]
         if s == NZ // 2:
-            pairs = pairs[i:i + 1]
+            half = panel.at[hop, blocks[0], xx, pl.ds(2 * (i % 2), 1)], panel.at[hop, blocks[1], xx, pl.ds(2 * (i % 2) + 1, 1)]
+            pairs = [(half[0], zp), (half[1], zm)]
         rings[hop, i, s] = [remote(block, block, peer) for block, peer in pairs]
         for copy in rings[hop, i, s]:
             copy.start()
+        if i == 0 and s > 1:
+            cross(hop, s - 1)
+
+    def cross(hop, s):
+        part_of = pl.ds(0, 2)
+        blocks = [rem(z - s, NZ), rem(z + s, NZ)]
+        if s == NZ // 2:
+            blocks = blocks[:1]
+        crossed[hop, s] = [remote(panel.at[hop, b, x, part_of], panel.at[hop, b, x, part_of], at(z, y, 1 - x)) for b in blocks]
+        for copy in crossed[hop, s]:
+            copy.start()
+
+    def ring_end(hop, i):
+        for copy in rings[hop, i, NZ // 2]:
+            copy.wait_recv()
+        if i == 0:
+            cross(hop, NZ // 2)
+
+    def cross_wait(hop, s):
+        blocks = [rem(z - s, NZ), rem(z + s, NZ)]
+        for b, copy in zip(blocks, crossed[hop, s]):
+            landed(panel.at[hop, b, 1 - x, pl.ds(0, 2)], copy)
 
     def ring_products(hop, i, s):
         xx = 1 - x if i else x
@@ -180,23 +205,31 @@
 
     forward = {}
 
-    def forward_core(hop):
-        for i in range(2):
-            fsend1[hop, i] = acc[rows_of((2 * i + 1 - core) * T, T), :]
-        forward["core", hop] = remote(fsend1.at[hop], frecv1.at[hop], c_core)
-        forward["core", hop].start()
-
-    def forward_far(hop):
-        forward["core", hop].wait_recv()
-        fsend2[hop] = acc[rows_of((2 * (1 - xh) + core) * T, T), :] + frecv1[hop, 1 - xh]
-        forward["far", hop] = remote(fsend2.at[hop], frecv2.at[hop], c_xh)
-        forward["far", hop].start()
+    def pack_tile(msg, a):
+        m = jnp.max(jnp.abs(a).reshape(T // 8, 8, T), axis=0)
+        e = jnp.ceil(jnp.log2(jnp.maximum(jnp.max(m, axis=0, keepdims=True), 1e-30)))
+        msg[pl.ds(T, PAD), :] = jnp.broadcast_to(e, (PAD, T)).astype(jnp.int32).astype(jnp.int16)
+        scale = jnp.broadcast_to(jnp.exp2(14.0 - e), (8, T))[None]
+        a = jnp.round(a.reshape(T // 8, 8, T) * scale).reshape(T, T)
+        msg[pl.ds(0, T), :] = a.astype(jnp.int32).astype(jnp.int16)
+
+    def forward_send(hop):
+        targets = ((c_far, (1 - xh) * 2 + 1 - core), (c_xh, (1 - xh) * 2 + core), (c_core, xh * 2 + 1 - core))
+        forward[hop] = []
+        for k, (peer, q) in enumerate(targets):
+            pack_tile(s_cols.at[hop, k], acc[rows_of(q * T, T), :])
+            copy = remote(s_cols.at[hop, k], r_cols.at[hop, k], peer)
+            copy.start()
+            forward[hop].append(copy)
 
     def forward_end(hop):
-        mine = acc[rows_of((2 * xh + core) * T, T), :] + frecv1[hop, xh]
+        mine = acc[rows_of(c * T, T), :]
         t_col = jnp.transpose(jnp.broadcast_to(t_row, (T, T)))
-        forward["far", hop].wait_recv()
-        mine = (1.0 - t_col) * (mine + frecv2[hop]) + t_col * h[...]
+        for k in (2, 1, 0):
+            forward[hop][k].wait_recv()
+            msg = r_cols.at[hop, k]
+            mine = mine + decode(msg, 0, scale_of(msg, T))
+        mine = (1.0 - t_col) * mine + t_col * h[...]
         if hop == 0:
             panel[1, z, x, y] = mine.astype(jnp.bfloat16)
         else:
@@ -306,7 +339,7 @@
     plane_start(0)
     query_start(0)
     load.wait()
-    tv[SLOTS] = jnp.zeros((T, T), jnp.bfloat16)
+    tv[0] = jnp.zeros((T, T), jnp.bfloat16)
 
     def fill(g, carry):
         for q in range(COLS):
@@ -317,57 +350,71 @@
     lax.fori_loop(0, GROUPS, fill, 0)
 
     p = PARTS
-    query_wait(0)
     acc[...] = jnp.zeros_like(acc)
-    for hop in range(2):
+
+    def ring_begin(hop):
         plane_wait(hop, 0)
         ring(hop, 0, 1)
+        ring(hop, 1, 1)
         plane_wait(hop, 1)
-        ring(hop, 1, 1)
+        ring(hop, 3, 1)
+
+    ring_begin(0)
+    query_wait(0)
+    for hop in range(2):
         if hop == 0:
             reduce_one(hop, p[0])
             reduce_one(hop, p[1])
         ring_products(hop, 0, 0)
         ring(hop, 0, 2)
+        ring(hop, 1, 2)
         if hop == 0:
             reduce_one(hop, p[2])
             reduce_one(hop, p[3])
-        ring(hop, 1, 2)
+        ring(hop, 3, 2)
         reduce_two(hop, p[0])
         reduce_two(hop, p[1])
+        ring(hop, 0, 3)
+        ring(hop, 1, 3)
         ring_products(hop, 1, 0)
         ring_products(hop, 0, 1)
+        ring(hop, 3, 3)
+        reduce_two(hop, p[2])
+        reduce_x(hop, p[0])
+        ring(hop, 0, 4)
+        ring(hop, 1, 4)
+        reduce_two(hop, p[3])
+        cross_wait(hop, 1)
         ring_products(hop, 1, 1)
-        ring(hop, 0, 3)
-        reduce_two(hop, p[2])
-        ring(hop, 1, 3)
-        reduce_x(hop, p[0])
-        reduce_two(hop, p[3])
         ring_products(hop, 0, 2)
+        ring(hop, 3, 4)
+        reduce_x(hop, p[1])
+        reduce_own(hop, p[0])
+        cross_wait(hop, 2)
         ring_products(hop, 1, 2)
-        reduce_x(hop, p[1])
-        ring(hop, 0, 4)
-        reduce_own(hop, p[0])
-        ring(hop, 1, 4)
+        ring_products(hop, 0, 3)
+        ring_end(hop, 0)
         reduce_x(hop, p[2])
         reduce_own(hop, p[1])
-        ring_products(hop, 0, 3)
+        ring_end(hop, 1)
+        cross_wait(hop, 3)
         ring_products(hop, 1, 3)
+        ring_products(hop, 0, 4)
         reduce_x(hop, p[3])
         reduce_own(hop, p[2])
-        for i in range(2):
-            rings[hop, i, 4][0].wait_recv()
-            ring_products(hop, i, 4)
-        forward_core(hop)
+        ring_end(hop, 3)
+        cross_wait(hop, 4)
+        ring_products(hop, 1, 4)
+        forward_send(hop)
         reduce_own(hop, p[3])
-        forward_far(hop)
-        adjoint_end(hop)
-        if hop == 0:
-            query_start(1)
         forward_end(hop)
         if hop == 0:
             plane_start(1)
             acc[...] = jnp.zeros_like(acc)
+        adjoint_end(hop)
+        if hop == 0:
+            query_start(1)
+            ring_begin(1)
             query_wait(1)
             for j in p:
                 reduce_one(1, j)
@@ -379,17 +426,16 @@
 
 
 def shards(h_start, cotangent, node_type, teleport, tile_values, tile_row, tile_col, tile_count):
-    k = tile_col[0, 0]
-    place = tile_row[0, 0] * 64 + (k // 8 * 2 + k % 2) * 4 + (k // 2) % 4
-    slot = jnp.arange(SLOTS, dtype=jnp.int32)
-    place = jnp.where(slot < tile_count[0, 0], place, -1)
-    hit = place[None, :] == jnp.arange(COLS * 64, dtype=jnp.int32)[:, None]
-    inv = SLOTS + jnp.sum(jnp.where(hit, slot[None, :] - SLOTS, 0), axis=1)
+    spot = jnp.arange(COLS * 64, dtype=jnp.int32)[:, None]
+    row, col = spot // 64, spot % 64 // 8 * 8 + spot % 4 * 2 + spot // 4 % 2
+    slot = jnp.arange(SLOTS, dtype=jnp.int32)[None, :]
+    hit = (tile_row[0] == row) & (tile_col[0] == col) & (slot < tile_count)
+    inv = jnp.sum(jnp.where(hit, slot + 1, 0), axis=1)
 
     vmem = pl.BlockSpec(memory_space=pltpu.VMEM)
     smem = pl.BlockSpec(memory_space=pltpu.SMEM)
     tile = jax.ShapeDtypeStruct((T, T), jnp.float32)
-    copies = 96
+    copies = 160
     return pl.pallas_call(
         kernel,
         out_shape=(tile, tile),
@@ -402,10 +448,8 @@
             pltpu.VMEM((64 * T, T), jnp.float32),
             pltpu.VMEM((2, T, COLS * T), jnp.bfloat16),
             pltpu.VMEM((COLS * T, T), jnp.float32),
-            pltpu.VMEM((2, 2, T, T), jnp.float32),
-            pltpu.VMEM((2, 2, T, T), jnp.float32),
-            pltpu.VMEM((2, T, T), jnp.float32),
-            pltpu.VMEM((2, T, T), jnp.float32),
+            pltpu.VMEM((2, 3, T + PAD, T), jnp.int16),
+            pltpu.VMEM((2, 3, T + PAD, T), jnp.int16),
             pltpu.VMEM((2, 4, 2, 2 * T + PAD, T), jnp.int16),
             pltpu.VMEM((2, 4, 2, 2 * T + PAD, T), jnp.int16),
             pltpu.VMEM((2, 4, 2, 4 * T + PAD, T), jnp.int16),

time: 97.9 us -> 90.5 us (0.924)
  Pallas kernels: 91.3 us -> 84.1 us
    pallas_call x1, Pallas kernels: 91.3 us -> 84.1 us  [shards(): pl.pallas_call(kernel, out_shape=(tile, tile), in_specs=[smem, smem, pl.B...]
    reduce_sum x1, other arithmetic: 0.13 us -> 1.44 us  [shards(): inv = jnp.sum(jnp.where(hit, slot + 1, 0), axis=1)]
where the time goes in v3:
time: 90.5 us; the launch traced here: 89.8 us
  Pallas kernels  84.1 us (93%)
  local copies, waits for them, and re-layouts  2.95 us (3%)
  other arithmetic  1.46 us (2%)
  between operations  1.3 us (1%)
    pallas_call x1, Pallas kernels, shards(): pl.pallas_call(kernel, out_shape=(tile, tile), in_specs=[smem, smem, pl.B...  84.1 us
    unnamed x2, local copies, waits for them, and re-layouts  2.95 us

profile of v3, /device:TPU:1, one launch (start us, length us, event | category | flops | bytes accessed | tf_op | source)
XLA Modules:
  0.0 89.8 jit_solution(7111703367742878447)
XLA Ops:
  1.3 1.4 %select_reduce_fusion.inv = s32[256]{0:T(256)} fusion(s32[192]{0:T(256)S(1)} %iota_add_fusion, s32[256]{0:T(256)S(1)} %get-tuple-element.3, s32[256]{0:T(256)S(1)} %get-tuple-element.2, s32[192]{0:T(256)} %bitcast.7, s32[192]{0:T(256)} %bitcast.8, pred[192]{0:T(512)(128)(4,1)S(1)} %iota_compare_fusion), kind=kLoop, calls=%fused_computation | loop fusion | flops 294656 | bytes 5568 | tf_op jit(solution)/shard_map/reduce_sum | solution.py:433
  2.8 84.1 %shard_map.95 = (f32[128,128]{1,0:T(8,128)}, f32[128,128]{1,0:T(8,128)}) custom-call(s32[256]{0:T(256)} %select_reduce_fusion.inv, f32[8]{0:T(128)} %rates.1, bf16[192,128,128]{2,1,0:T(8,128)(2,1)} %bitcast.6, f32[128,128]{1,0:T(8,128)} %h.1, f32[128,128]{1,0:T(8,128)} %cot.1, s32[1,128]{1,0:T(1,128)} %bitcast.9), custom_call_target="tpu_custom_call" | custom-call | tf_op jit(solution)/shard_map/pallas_call | solution.py:439
  86.9 1.5 %copy.13 = f32[128,128]{1,0:T(8,128)} copy(f32[128,128]{1,0:T(8,128)} %get-tuple-element.6) | data formatting | bytes 131072
  88.3 1.5 %copy.14 = f32[128,128]{1,0:T(8,128)} copy(f32[128,128]{1,0:T(8,128)} %get-tuple-element.7) | data formatting | bytes 131072
  (3 shorter events, 0.0 us)

commit v4 on v3

--- a/solution.py
+++ b/solution.py
@@ -315,19 +315,14 @@
                     pl.when(slot != 0)(copy.wait_send)
 
     def adjoint_end(hop):
-        for slot in range(1, NZ):
+        row = tile_row(0, z, x)
+        for slot in (4, 3, 5, 2, 6, 7, 1):
             pltpu.make_async_remote_copy(
                 src_ref=r_own.at[hop, slot], dst_ref=r_own.at[hop, slot], send_sem=so.at[hop, 0],
                 recv_sem=ro.at[hop, slot], device_id=yp, device_id_type=MESH,
             ).wait_recv()
-
-        row = tile_row(0, z, x)
-
-        def one(slot, carry):
             add_message(r_own.at[hop, slot], row, 1)
-            return carry
-
-        lax.fori_loop(1, NZ, one, 0)
+
         d = part[rows_of(row, T), :]
         if hop == 0:
             d_one[...] = d
@@ -407,13 +402,13 @@
         ring_products(hop, 1, 4)
         forward_send(hop)
         reduce_own(hop, p[3])
+        adjoint_end(hop)
+        if hop == 0:
+            query_start(1)
         forward_end(hop)
         if hop == 0:
             plane_start(1)
             acc[...] = jnp.zeros_like(acc)
-        adjoint_end(hop)
-        if hop == 0:
-            query_start(1)
             ring_begin(1)
             query_wait(1)
             for j in p:
@@ -423,6 +418,11 @@
         copy.wait_send()
     for hop in range(2):
         own_done(hop)
+
+
+def hand_over(a, b, prop, grad):
+    prop[...] = a[...]
+    grad[...] = b[...]
 
 
 def shards(h_start, cotangent, node_type, teleport, tile_values, tile_row, tile_col, tile_count):
@@ -436,7 +436,7 @@
     smem = pl.BlockSpec(memory_space=pltpu.SMEM)
     tile = jax.ShapeDtypeStruct((T, T), jnp.float32)
     copies = 160
-    return pl.pallas_call(
+    raw = pl.pallas_call(
         kernel,
         out_shape=(tile, tile),
         in_specs=[smem, smem, pl.BlockSpec(memory_space=pl.ANY)] + [vmem] * 3,
@@ -469,6 +469,12 @@
             collective_id=0, has_side_effects=True, vmem_limit_bytes=56 << 20
         ),
     )(inv, teleport, tile_values[0, 0], h_start, cotangent, node_type[None, :])
+    return pl.pallas_call(
+        hand_over,
+        out_shape=(tile, tile),
+        in_specs=[vmem, vmem],
+        out_specs=(vmem, vmem),
+    )(*raw)
 
 
 def solution(mesh):

time: 90.5 us -> 88.4 us (0.977)
  local copies, waits for them, and re-layouts: 2.95 us -> 0 us
  Pallas kernels: 84.1 us -> 85.4 us
    unnamed x2 -> x0, local copies, waits for them, and re-layouts: 2.95 us -> none
    pallas_call x0 -> x1, Pallas kernels: none -> 1.53 us  [shards(): pl.pallas_call(hand_over, out_shape=(tile, tile), in_specs=[vmem, vmem],...]
where the time goes in v4:
time: 88.4 us; the launch traced here: 88.2 us
  Pallas kernels  85.4 us (97%)
  other arithmetic  1.46 us (2%)
  between operations  1.3 us (1%)
    pallas_call x1, Pallas kernels, shards(): pl.pallas_call(kernel, out_shape=(tile, tile), in_specs=[smem, smem, pl.B...  83.9 us

profile of v4, /device:TPU:1, one launch (start us, length us, event | category | flops | bytes accessed | tf_op | source)
XLA Modules:
  0.0 88.2 jit_solution(14467894280451234731)
XLA Ops:
  1.3 1.4 %select_reduce_fusion.inv = s32[256]{0:T(256)} fusion(s32[192]{0:T(256)S(1)} %iota_add_fusion, s32[256]{0:T(256)S(1)} %get-tuple-element.7, s32[256]{0:T(256)S(1)} %get-tuple-element.6, s32[192]{0:T(256)} %bitcast.7, s32[192]{0:T(256)} %bitcast.8, pred[192]{0:T(512)(128)(4,1)S(1)} %iota_compare_fusion), kind=kLoop, calls=%fused_computation | loop fusion | flops 294656 | bytes 5568 | tf_op jit(solution)/shard_map/reduce_sum | solution.py:433
  2.8 83.9 %shard_map.95 = (f32[128,128]{1,0:T(8,128)}, f32[128,128]{1,0:T(8,128)}) custom-call(s32[256]{0:T(256)} %select_reduce_fusion.inv, f32[8]{0:T(128)} %rates.1, bf16[192,128,128]{2,1,0:T(8,128)(2,1)} %bitcast.6, f32[128,128]{1,0:T(8,128)} %h.1, f32[128,128]{1,0:T(8,128)} %cot.1, s32[1,128]{1,0:T(1,128)} %bitcast.9), custom_call_target="tpu_custom_call" | custom-call | tf_op jit(solution)/shard_map/pallas_call | solution.py:439
  86.7 1.5 %shard_map.96 = (f32[128,128]{1,0:T(8,128)}, f32[128,128]{1,0:T(8,128)}) custom-call(f32[128,128]{1,0:T(8,128)} %get-tuple-element.4.a, f32[128,128]{1,0:T(8,128)} %get-tuple-element.5.b), custom_call_target="tpu_custom_call" | custom-call | tf_op jit(solution)/shard_map/pallas_call | solution.py:472
  (3 shorter events, 0.0 us)

commit v5 on v4

--- a/solution.py
+++ b/solution.py
@@ -396,12 +396,12 @@
         ring_products(hop, 1, 3)
         ring_products(hop, 0, 4)
         reduce_x(hop, p[3])
+        ring_end(hop, 3)
         reduce_own(hop, p[2])
-        ring_end(hop, 3)
+        reduce_own(hop, p[3])
         cross_wait(hop, 4)
         ring_products(hop, 1, 4)
         forward_send(hop)
-        reduce_own(hop, p[3])
         adjoint_end(hop)
         if hop == 0:
             query_start(1)

time: 88.4 us -> 91.6 us (1.036)
  Pallas kernels: 85.4 us -> 88.6 us
    pallas_call x1, Pallas kernels: 83.9 us -> 87.1 us  [shards(): pl.pallas_call(kernel, out_shape=(tile, tile), in_specs=[smem, smem, pl.B...]
where the time goes in v5:
time: 91.6 us; the launch traced here: 91.4 us
  Pallas kernels  88.6 us (97%)
  other arithmetic  1.46 us (2%)
  between operations  1.3 us (1%)
    pallas_call x1, Pallas kernels, shards(): pl.pallas_call(kernel, out_shape=(tile, tile), in_specs=[smem, smem, pl.B...  87.1 us

profile of v5, /device:TPU:1, one launch (start us, length us, event | category | flops | bytes accessed | tf_op | source)
XLA Modules:
  0.0 91.4 jit_solution(12039809926577474335)
XLA Ops:
  1.3 1.4 %select_reduce_fusion.inv = s32[256]{0:T(256)} fusion(s32[192]{0:T(256)S(1)} %iota_add_fusion, s32[256]{0:T(256)S(1)} %get-tuple-element.7, s32[256]{0:T(256)S(1)} %get-tuple-element.6, s32[192]{0:T(256)} %bitcast.7, s32[192]{0:T(256)} %bitcast.8, pred[192]{0:T(512)(128)(4,1)S(1)} %iota_compare_fusion), kind=kLoop, calls=%fused_computation | loop fusion | flops 294656 | bytes 5568 | tf_op jit(solution)/shard_map/reduce_sum | solution.py:433
  2.8 87.1 %shard_map.95 = (f32[128,128]{1,0:T(8,128)}, f32[128,128]{1,0:T(8,128)}) custom-call(s32[256]{0:T(256)} %select_reduce_fusion.inv, f32[8]{0:T(128)} %rates.1, bf16[192,128,128]{2,1,0:T(8,128)(2,1)} %bitcast.6, f32[128,128]{1,0:T(8,128)} %h.1, f32[128,128]{1,0:T(8,128)} %cot.1, s32[1,128]{1,0:T(1,128)} %bitcast.9), custom_call_target="tpu_custom_call" | custom-call | tf_op jit(solution)/shard_map/pallas_call | solution.py:439
  89.8 1.5 %shard_map.96 = (f32[128,128]{1,0:T(8,128)}, f32[128,128]{1,0:T(8,128)}) custom-call(f32[128,128]{1,0:T(8,128)} %get-tuple-element.4.a, f32[128,128]{1,0:T(8,128)} %get-tuple-element.5.b), custom_call_target="tpu_custom_call" | custom-call | tf_op jit(solution)/shard_map/pallas_call | solution.py:472
  (3 shorter events, 0.0 us)
